TPU v7x, 32 devices: a whole 2x2x4 slice. The times are simulated.
32 devices in a mesh: section: 4 (over y, x), dp: 8 (over z, core).
Axes of the slice: x: 2, y: 2, z: 4, core: 2. Of those that a mesh axis runs over, the one named last changes fastest.
Arguments:
- saved_states: bfloat16 [4, 2, 128, 2688], P('section', None, 'dp'), may hold values from -64 to 64
- cotangent_in: bfloat16 [4, 128, 2688], P('section', 'dp'), may hold values from -6 to 6
- lengths: int32 [4], P('section'), may hold values from 16 to 128
- gain: bfloat16 [2688], replicated, may hold values from 0.099609375 to 1.8984375
- up_weight: bfloat16 [2688, 9216], P('section', 'dp'), may hold values from -0.125 to 0.125
- down_weight: bfloat16 [9216, 2688], P('dp', 'section'), may hold values from -0.0625 to 0.0625
Outputs:
- cotangent_out: bfloat16 [4, 128, 2688], P('section', 'dp')
- up_gradient: bfloat16 [2688, 9216], P('section', 'dp')
- down_gradient: bfloat16 [9216, 2688], P('dp', 'section')
- gain_gradient: float32 [2688], replicated
All inputs are finite; a program needn't handle non-finite values.
Results may differ from a plain program's by a relative error of at most 0.024.
Values may be sent and summed in bfloat16 or wider, within the bound.
No kernel may reach another device: no remote copies, remote signals or barrier semaphores. Data moves between devices by JAX's collectives and lax.ppermute only.
A program may use at most 64 MiB of HBM per device.

v0:
```python
import math
import jax
import jax.numpy as jnp
from jax import lax
from jax.sharding import PartitionSpec as P

epsilon = 1e-06


def passed_along(block, axis, distance):
    devices = range(lax.axis_size(axis))
    route = [((i - distance) % len(devices), i) for i in devices]
    return lax.ppermute(block, axis, route)


def back_iteration(state, cotangent, gain, up_full, down_full, member, share):
    values = state.astype(jnp.float32)
    reciprocal = lax.rsqrt(jnp.mean(values * values, axis=-1, keepdims=True) + epsilon)
    scaled = values * reciprocal
    gain_wide = gain.astype(jnp.float32)
    normed = (scaled * gain_wide).astype(jnp.bfloat16)
    hidden_in = jnp.dot(normed, up_full, preferred_element_type=jnp.float32)
    sigma = jax.nn.sigmoid(hidden_in)
    hidden_out = (hidden_in * sigma).astype(jnp.bfloat16)
    back_out = lax.dot_general(
        cotangent, down_full, (((1,), (1,)), ((), ())), preferred_element_type=jnp.float32
    )
    back_in = (back_out * sigma * (1.0 + hidden_in * (1.0 - sigma))).astype(jnp.bfloat16)
    partial_value = lax.dot_general(
        back_in, up_full, (((1,), (1,)), ((), ())), preferred_element_type=jnp.float32
    )
    back_normed = lax.psum_scatter(
        partial_value.astype(jnp.bfloat16), "dp", scatter_dimension=0, tiled=True
    ).astype(jnp.float32)
    start = member * share
    rows_scaled = lax.dynamic_slice_in_dim(scaled, start, share, 0)
    rows_recip = lax.dynamic_slice_in_dim(reciprocal, start, share, 0)
    rows_cot = lax.dynamic_slice_in_dim(cotangent, start, share, 0)
    gained = back_normed * gain_wide
    back_state = rows_recip * (
        gained - rows_scaled * jnp.mean(gained * rows_scaled, axis=-1, keepdims=True)
    )
    result = (rows_cot.astype(jnp.float32) + back_state).astype(jnp.bfloat16)
    gain_term = jnp.sum(back_normed * rows_scaled, axis=0)
    return (result, normed, back_in, hidden_out, gain_term)


def hand_over(result):
    arrived = passed_along(result, "section", -1)
    return lax.all_gather(arrived, "dp", axis=0, tiled=True)


def contract_rows(left, right):
    return lax.dot_general(
        left, right, (((0,), (0,)), ((), ())), preferred_element_type=jnp.float32
    )


def reduce_terms(up_terms, down_terms):
    return (
        lax.psum_scatter(
            up_terms.astype(jnp.bfloat16), "section", scatter_dimension=0, tiled=True
        ).astype(jnp.float32),
        lax.psum_scatter(
            down_terms.astype(jnp.bfloat16), "section", scatter_dimension=1, tiled=True
        ).astype(jnp.float32),
    )


def on_device(saved_states, cotangent_in, lengths, gain, up_weight, down_weight):
    up_full, down_full = (
        lax.all_gather(up_weight, "section", axis=0, tiled=True),
        lax.all_gather(down_weight, "section", axis=1, tiled=True),
    )
    group_states, group_cotangent = (
        lax.all_gather(saved_states, "dp", axis=2, tiled=True),
        lax.all_gather(cotangent_in, "dp", axis=1, tiled=True),
    )
    turns = group_states.shape[1]
    tokens = group_states.shape[2]
    share = saved_states.shape[2]
    member = lax.axis_index("dp")
    positions = lax.broadcasted_iota(jnp.int32, (tokens, 1), 0)
    cotangent = jnp.where(
        positions < lengths[0], group_cotangent[0], jnp.zeros_like(group_cotangent[0])
    )
    scale = 1.0 / math.sqrt(turns * tokens * lax.axis_size("section"))
    gain_total = jnp.zeros((gain.shape[0],), jnp.float32)
    up_total = jnp.zeros(up_full.shape, jnp.float32)
    down_total = jnp.zeros(down_full.shape, jnp.float32)
    result = cotangent
    for turn in range(turns):
        if turn > 0:
            cotangent = hand_over(result)
        result, normed, back_in, hidden_out, gain_term = back_iteration(
            group_states[0, turn], cotangent, gain, up_full, down_full, member, share
        )
        gain_total = gain_total + gain_term
        up_total = up_total + contract_rows(normed, back_in)
        down_total = down_total + contract_rows(hidden_out, cotangent)
    up_sum, down_sum = reduce_terms(up_total * scale, down_total * scale)
    gain_sum = lax.psum(gain_total * scale, ("section", "dp"))
    own_rows = result[None]
    return (own_rows, up_sum.astype(jnp.bfloat16), down_sum.astype(jnp.bfloat16), gain_sum)


def solution(mesh):
    placed = (
        P("section", None, "dp", None),
        P("section", "dp", None),
        P("section"),
        P(),
        P("section", "dp"),
        P("dp", "section"),
    )
    return jax.shard_map(
        on_device,
        mesh=mesh,
        in_specs=placed,
        out_specs=(P("section", "dp", None), P("section", "dp"), P("dp", "section"), P()),
        check_vma=False,
    )
```

profile of v0, /device:TPU:0, one launch (start us, length us, event | category | flops | bytes accessed | tf_op | source)
XLA Modules:
  0.0 431.3 jit_solution(11454074368772299027)
XLA Ops:
  7.2 0.0 all-gather.4.cloned.1.call-start
  7.2 0.7 all-gather.4.cloned.1.call-update
  7.9 0.0 copy-start.7
  7.9 0.0 copy-start.5
  7.9 0.0 all-gather.8.cloned.1.call-start
  8.0 0.7 all-gather.8.cloned.1.call-update
  8.7 0.0 all-gather.6.cloned.1.call-start
  8.7 0.7 all-gather.6.cloned.1.call-update
  9.4 0.0 reduce-scatter.5.cloned.1.call-start
  10.1 0.0 copy-done.7
  10.1 0.0 copy-done.5
  10.1 18.4 %all_gather.15 = bf16[1,128,2688]{2,1,0:T(8,128)(2,1)S(1)} all-gather(bf16[1,16,2688]{2,1,0:T(8,128)(2,1)S(1)} %copy-done.5), channel_id=1, replica_groups=mesh['section'=4,'dp'=8] {'dp'}, dimensions={1}, use_global_device_ids=true | all-gather | bytes 774144 | tf_op jit(solution)/shard_map/all_gather | solution.py:77
  28.5 0.1 bitcast_select_fusion
  28.7 0.0 copy-start.2
  28.7 8.8 %all-gather.4.cloned.1.call-done = bf16[1,2,128,2688]{3,2,1,0:T(8,128)(2,1)} async-done(((bf16[1,2,16,2688]{3,2,1,0:T(8,128)(2,1)}), bf16[1,2,128,2688]{3,2,1,0:T(8,128)(2,1)}) %all-gather.4.cloned.1.call-update) | async-done | bytes 1376272 | tf_op jit(solution)/shard_map/all_gather | solution.py:76
  37.4 0.0 copy-start.1
  37.4 1.8 fusion.8
  39.2 68.8 %all-gather.8.cloned.1.call-done = bf16[2688,1152]{1,0:T(8,128)(2,1)} async-done(((bf16[672,1152]{1,0:T(8,128)(2,1)}), bf16[2688,1152]{1,0:T(8,128)(2,1)}) %all-gather.8.cloned.1.call-update) | async-done | bytes 6193168 | tf_op jit(solution)/shard_map/all_gather | solution.py:72
  108.0 0.0 copy-done.1
  108.0 3.9 fusion.14
  111.9 67.2 %all-gather.6.cloned.1.call-done = bf16[1152,2688]{0,1:T(8,128)(2,1)} async-done(((bf16[1152,672]{0,1:T(8,128)(2,1)}), bf16[1152,2688]{0,1:T(8,128)(2,1)}) %all-gather.6.cloned.1.call-update) | async-done | bytes 6193168 | tf_op jit(solution)/shard_map/all_gather | solution.py:73
  179.1 4.1 fusion.6
  183.2 0.5 copy-done
  183.7 2.8 convolution_convert_fusion.1
  186.4 0.0 reduce-scatter.5.cloned.1.call-update
  186.5 0.0 reduce-scatter.7.cloned.1.call-start
  186.5 0.1 dynamic-slice.6
  186.6 1.8 convert_multiply_fusion.2
  188.4 0.0 copy-done.8
  188.4 30.0 %reduce-scatter.5.cloned.1.call-done = bf16[16,2688]{1,0:T(8,128)(2,1)} async-done(((bf16[128,2688]{1,0:T(8,128)(2,1)}), bf16[16,2688]{1,0:T(8,128)(2,1)}) %reduce-scatter.5.cloned.1.call-update) | async-done | bytes 86032 | tf_op jit(solution)/shard_map/reduce_scatter | solution.py:32
  218.4 1.6 fusion.28
  220.0 0.0 copy-done.2
  220.0 1.1 fusion.27
  221.1 2.4 collective-permute-start
  223.5 4.1 fusion.15
  227.5 0.0 collective-permute-done
  227.5 15.4 %all_gather.19 = bf16[128,2688]{1,0:T(8,128)(2,1)S(1)} all-gather(bf16[16,2688]{1,0:T(8,128)(2,1)S(1)} %collective-permute-done), channel_id=1, replica_groups=mesh['section'=4,'dp'=8] {'dp'}, dimensions={0}, use_global_device_ids=true | all-gather | bytes 774144 | tf_op jit(solution)/shard_map/all_gather | solution.py:50
  243.0 4.1 fusion.7
  247.1 0.0 copy-start.3
  247.1 0.7 copy-done.3
  247.8 0.0 slice-done
  247.8 0.0 slice-done.1
  247.8 2.8 convolution_convert_fusion
  250.6 0.0 reduce-scatter.7.cloned.1.call-update
  250.6 0.2 reduce-scatter.11.cloned.1.call-start
  250.8 2.9 fusion.10
  253.8 4.6 %fusion.2 = bf16[1152,2688]{0,1:T(8,128)(2,1)} fusion(f32[1152,2688]{0,1:T(8,128)S(1)} %fusion.10, bf16[128,2688]{1,0:T(8,128)(2,1)S(1)} %all_gather.19, f32[128,1152]{1,0:T(8,128)S(1)} %fusion.15), kind=kOutput, calls=%fused_computation.4 | convolution fusion | flops 802750464 | bytes 19857408 | tf_op jit(solution)/shard_map/dot_general | solution.py:54
  258.3 0.0 reduce-scatter.11.cloned.1.call-update
  258.4 0.0 copy-start.4
  258.4 0.0 copy-start.9
  258.4 0.0 reduce-scatter.9.cloned.1.call-start
  258.4 1.9 fusion.13
  260.3 0.0 copy-done.4
  260.3 0.0 copy-done.9
  260.3 4.5 %fusion.3 = bf16[2688,1152]{1,0:T(8,128)(2,1)} fusion(f32[2688,1152]{1,0:T(8,128)S(1)} %fusion.13, bf16[128,1152]{1,0:T(8,128)(2,1)S(1)} %copy-done.4, f32[2688]{0:T(1024)S(1)} %convert_element_type.71, f32[128]{0:T(128)S(1)} %copy-done.9, bf16[1,2,128,2688]{3,2,1,0:T(8,128)(2,1)S(1)} %copy-done.1), kind=kOutput, calls=%fused_computation.5 | convolution fusion | flops 803389440 | bytes 19575296 | tf_op jit(solution)/shard_map/dot_general | solution.py:54
  264.9 0.0 reduce-scatter.9.cloned.1.call-update
  264.9 0.1 dynamic-slice.7
  265.0 14.7 %reduce-scatter.7.cloned.1.call-done = bf16[16,2688]{1,0:T(8,128)(2,1)} async-done(((bf16[128,2688]{1,0:T(8,128)(2,1)}), bf16[16,2688]{1,0:T(8,128)(2,1)}) %reduce-scatter.7.cloned.1.call-update) | async-done | bytes 86032 | tf_op jit(solution)/shard_map/reduce_scatter | solution.py:32
  279.7 1.1 fusion.29
  280.8 0.0 copy-done.6
  280.9 38.9 %psum.7 = f32[2688]{0:T(1024)} all-reduce(f32[2688]{0:T(1024)S(1)} %add_multiply_fusion), channel_id=1, replica_groups=mesh['section'=4,'dp'=8] {'section','dp'}, use_global_device_ids=true, to_apply=%region_10.11 | all-reduce | flops 2688 | bytes 21504 | tf_op jit(solution)/shard_map/psum | solution.py:102
  319.8 1.7 fusion.30
  321.5 30.1 %reduce-scatter.11.cloned.1.call-done = bf16[1152,672]{0,1:T(8,128)(2,1)} async-done(((bf16[1152,2688]{0,1:T(8,128)(2,1)}), bf16[1152,672]{0,1:T(8,128)(2,1)}) %reduce-scatter.11.cloned.1.call-update) | async-done | bytes 1548304 | tf_op jit(solution)/shard_map/reduce_scatter | solution.py:64
  351.5 72.9 %reduce-scatter.9.cloned.1.call-done = bf16[672,1152]{1,0:T(8,128)(2,1)} async-done(((bf16[2688,1152]{1,0:T(8,128)(2,1)}), bf16[672,1152]{1,0:T(8,128)(2,1)}) %reduce-scatter.9.cloned.1.call-update) | async-done | bytes 1548304 | tf_op jit(solution)/shard_map/reduce_scatter | solution.py:61
  (13 shorter events, 0.0 us)
Async XLA Ops:
  7.2 30.3 %all-gather.4.cloned.1.call-start = ((), (), s32[]{:S(2)}) async-start(), calls=%async_computation.4 | async-start | bytes 1548288 | tf_op jit(solution)/shard_map/all_gather | solution.py:76
  7.9 2.2 copy-start.7
  7.9 2.2 copy-start.5
  7.9 100.1 %all-gather.8.cloned.1.call-start = ((), (), s32[]{:S(2)}) async-start(), calls=%async_computation.6 | async-start | bytes 7741440 | tf_op jit(solution)/shard_map/all_gather | solution.py:72
  8.7 170.4 %all-gather.6.cloned.1.call-start = ((), (), s32[]{:S(2)}) async-start(), calls=%async_computation.5 | async-start | bytes 7741440 | tf_op jit(solution)/shard_map/all_gather | solution.py:73
  9.4 209.0 %reduce-scatter.5.cloned.1.call-start = ((), (), s32[]{:S(2)}) async-start(), calls=%async_computation.7 | async-start | bytes 774144 | tf_op jit(solution)/shard_map/reduce_scatter | solution.py:32
  28.7 191.3 %copy-start.2 = (bf16[128,2688]{1,0:T(8,128)(2,1)}, bf16[128,2688]{1,0:T(8,128)(2,1)S(1)}, u32[]{:S(2)}) copy-start(bf16[128,2688]{1,0:T(8,128)(2,1)S(1)} %bitcast_select_fusion) | copy-start | bytes 2064388
  37.4 70.6 %copy-start.1 = (bf16[1,2,128,2688]{3,2,1,0:T(8,128)(2,1)S(1)}, bf16[1,2,128,2688]{3,2,1,0:T(8,128)(2,1)}, u32[]{:S(2)}) copy-start(bf16[1,2,128,2688]{3,2,1,0:T(8,128)(2,1)} %all-gather.4.cloned.1.call-done) | copy-start | bytes 4128772
  179.1 4.5 %copy-start = (bf16[2688,1152]{1,0:T(8,128)(2,1)S(1)}, bf16[2688,1152]{1,0:T(8,128)(2,1)}, u32[]{:S(2)}) copy-start(bf16[2688,1152]{1,0:T(8,128)(2,1)} %all-gather.8.cloned.1.call-done) | copy-start | bytes 18579460
  186.5 93.3 %reduce-scatter.7.cloned.1.call-start = ((), (), s32[]{:S(2)}) async-start(), calls=%async_computation.8 | async-start | bytes 774144 | tf_op jit(solution)/shard_map/reduce_scatter | solution.py:32
  186.6 1.8 copy-start.8
  221.1 6.5 %collective-permute-start = (bf16[16,2688]{1,0:T(8,128)(2,1)S(1)}, bf16[16,2688]{1,0:T(8,128)(2,1)S(1)}, u32[]{:S(2)}, u32[]{:S(2)}) collective-permute-start(bf16[16,2688]{1,0:T(8,128)(2,1)S(1)} %fusion.27), channel_id=1, source_target_pairs={{8,0},{16,8},{24,16},{0,24},{9,1},{17,9},{25,17},{1,25},{10,2},{18... | collective-permute-start | bytes 258056 | tf_op jit(solution)/shard_map/ppermute | solution.py:13
  223.5 24.3 %slice-start = ((s8[6193152]{0:T(1024)(128)(4,1)}), s8[4194304]{0:T(1024)(128)(4,1)S(1)}, s32[]{:S(2)}) async-start(s8[6193152]{0:T(1024)(128)(4,1)} %bitcast.46), calls=%async_computation.11 | async-start | bytes 8388608
  243.0 4.8 %slice-start.1 = ((s8[6193152]{0:T(1024)(128)(4,1)}), s8[1998848]{0:T(1024)(128)(4,1)S(1)}, s32[]{:S(2)}) async-start(s8[6193152]{0:T(1024)(128)(4,1)} %bitcast.46), calls=%async_computation.12 | async-start | bytes 3997696
  247.1 0.7 copy-start.3
  250.6 100.9 %reduce-scatter.11.cloned.1.call-start = ((), (), s32[]{:S(2)}) async-start(), calls=%async_computation.10 | async-start | bytes 7741440 | tf_op jit(solution)/shard_map/reduce_scatter | solution.py:64
  258.4 2.0 copy-start.4
  258.4 2.0 copy-start.9
  258.4 166.1 %reduce-scatter.9.cloned.1.call-start = ((), (), s32[]{:S(2)}) async-start(), calls=%async_computation.9 | async-start | bytes 7741440 | tf_op jit(solution)/shard_map/reduce_scatter | solution.py:61
  264.9 16.0 %copy-start.6 = (f32[2688]{0:T(1024)S(1)}, f32[2688]{0:T(1024)}, u32[]{:S(2)}) copy-start(f32[2688]{0:T(1024)} %get-tuple-element.6) | copy-start | bytes 32260
Sparse Core Ops, SparseCore 0:
  9.6 27.8 all-gather.3
  39.3 68.6 all-gather.7
  109.9 69.1 all-gather.5
  186.6 31.7 reduce-scatter.4
  250.7 28.9 reduce-scatter.6
  283.2 68.2 reduce-scatter.10
  355.2 69.2 reduce-scatter.8
where the time goes:
time: 432 us; the launch traced here: 431 us
  waiting for transfers between devices  295 us (68%)
  blocking collectives  72.7 us (17%)
  matrix products  35.6 us (8%)
  between operations  14.9 us (3%)
  other arithmetic  9.26 us (2%)
    reduce_scatter x1, waiting for transfers between devices, reduce_terms(): lax.psum_scatter(up_terms.astype(jnp.bfloat16), 'section', scatter_dimens...  72.9 us
    all_gather x1, waiting for transfers between devices, on_device(): lax.all_gather(up_weight, 'section', axis=0, tiled=True)  68.8 us
    all_gather x1, waiting for transfers between devices, on_device(): lax.all_gather(down_weight, 'section', axis=1, tiled=True)  67.2 us
    reduce_scatter x2, waiting for transfers between devices, back_iteration(): lax.psum_scatter(partial_value.astype(jnp.bfloat16), 'dp', scatter_dimens...  44.7 us
    psum x1, blocking collectives, on_device(): gain_sum = lax.psum(gain_total * scale, ('section', 'dp'))  38.9 us
    reduce_scatter x1, waiting for transfers between devices, reduce_terms(): lax.psum_scatter(down_terms.astype(jnp.bfloat16), 'section', scatter_dime...  30.1 us
    all_gather x1, blocking collectives, on_device(): lax.all_gather(cotangent_in, 'dp', axis=1, tiled=True)  18.4 us
    all_gather x1, blocking collectives, hand_over(): return lax.all_gather(arrived, 'dp', axis=0, tiled=True)  15.4 us
  transfers between devices with their start and end apart: 8, of which 7 were waited for; matrix products, arithmetic and copies ran while one was open for 7% of the time, Pallas kernels for 0%

commit v1 on v0

--- a/solution.py
+++ b/solution.py
@@ -1,3 +1,4 @@
+import functools
 import math
 import jax
 import jax.numpy as jnp
@@ -5,6 +6,19 @@
 from jax.sharding import PartitionSpec as P
 
 epsilon = 1e-06
+
+
+def scales_deliver(m, along_axis, d0):
+    low = jnp.concatenate(
+        jax.lax.all_to_all(
+            jnp.stack([m for _ in range(jax.lax.axis_size(along_axis))]), along_axis, 0, 0
+        ),
+        axis=d0,
+    )
+    return low
+
+
+begin_the_slot = functools.partial(scales_deliver, along_axis="section", d0=0)
 
 
 def passed_along(block, axis, distance):
@@ -69,7 +83,7 @@
 
 def on_device(saved_states, cotangent_in, lengths, gain, up_weight, down_weight):
     up_full, down_full = (
-        lax.all_gather(up_weight, "section", axis=0, tiled=True),
+        begin_the_slot(up_weight),
         lax.all_gather(down_weight, "section", axis=1, tiled=True),
     )
     group_states, group_cotangent = (

time: 432 us -> 403 us (0.933)
  waiting for transfers between devices: 295 us -> 249 us
  starting transfers between devices: 2.84 us -> 8.28 us
  local copies, waits for them, and re-layouts: 1.37 us -> 6.09 us
    all_gather x1 -> x0, waiting for transfers between devices: 68.8 us -> none  [on_device(): lax.all_gather(up_weight, 'section', axis=0, tiled=True)]
    all_to_all x0 -> x1, waiting for transfers between devices: none -> 60.6 us  [scales_deliver(): jax.lax.all_to_all(jnp.stack([m for _ in range(jax.lax.axis_size(along_ax...]
    reduce_scatter x1, waiting for transfers between devices: 72.9 us -> 30.1 us  [reduce_terms(): lax.psum_scatter(up_terms.astype(jnp.bfloat16), 'section', scatter_dimens...]
    reduce_scatter x1, waiting for transfers between devices: 30.1 us -> 72.8 us  [reduce_terms(): lax.psum_scatter(down_terms.astype(jnp.bfloat16), 'section', scatter_dime...]
    all_gather x1, waiting for transfers between devices: 67.2 us -> 37.5 us  [on_device(): lax.all_gather(down_weight, 'section', axis=1, tiled=True)]
    all_gather x1, waiting for transfers between devices: 8.75 us -> 2.39 us  [on_device(): lax.all_gather(saved_states, 'dp', axis=2, tiled=True)]
    dot_general x2, matrix products: 5.59 us -> 11.1 us  [back_iteration(): lax.dot_general(back_in, up_full, (((1,), (1,)), ((), ())), preferred_ele...]
    all_to_all x0 -> x1, starting transfers between devices: none -> 5.37 us  [scales_deliver(): jax.lax.all_to_all(jnp.stack([m for _ in range(jax.lax.axis_size(along_ax...]
  transfers between devices with their start and end apart: 8 -> 8, of which waited for: 7 -> 7; matrix products, arithmetic and copies ran while one was open for 7% -> 8% of each run, Pallas kernels for 0% -> 0%
where the time goes in v1:
time: 403 us
  waiting for transfers between devices  249 us (62%)
  blocking collectives  75.6 us (19%)
  matrix products  39.6 us (10%)
  between operations  14.9 us (4%)
  other arithmetic  9.22 us (2%)
  starting transfers between devices  8.28 us (2%)
  local copies, waits for them, and re-layouts  6.09 us (2%)
    reduce_scatter x1, waiting for transfers between devices, reduce_terms(): lax.psum_scatter(down_terms.astype(jnp.bfloat16), 'section', scatter_dime...  72.8 us
    all_to_all x1, waiting for transfers between devices, scales_deliver(): jax.lax.all_to_all(jnp.stack([m for _ in range(jax.lax.axis_size(along_ax...  60.6 us
    reduce_scatter x2, waiting for transfers between devices, back_iteration(): lax.psum_scatter(partial_value.astype(jnp.bfloat16), 'dp', scatter_dimens...  44.1 us
    psum x1, blocking collectives, on_device(): gain_sum = lax.psum(gain_total * scale, ('section', 'dp'))  38.9 us
    all_gather x1, waiting for transfers between devices, on_device(): lax.all_gather(down_weight, 'section', axis=1, tiled=True)  37.5 us
    reduce_scatter x1, waiting for transfers between devices, reduce_terms(): lax.psum_scatter(up_terms.astype(jnp.bfloat16), 'section', scatter_dimens...  30.1 us
    all_gather x1, blocking collectives, on_device(): lax.all_gather(cotangent_in, 'dp', axis=1, tiled=True)  21.3 us
    all_gather x1, blocking collectives, hand_over(): return lax.all_gather(arrived, 'dp', axis=0, tiled=True)  15.4 us
  transfers between devices with their start and end apart: 8, of which 7 were waited for; matrix products, arithmetic and copies ran while one was open for 8% of the time, Pallas kernels for 0%

profile of v1, /device:TPU:0, one launch (start us, length us, event | category | flops | bytes accessed | tf_op | source)
XLA Modules:
  0.0 402.5 jit_solution(16659409004208462910)
XLA Ops:
  7.2 0.0 copy-start.3
  7.2 0.0 all-gather.3.cloned.1.call-start
  7.2 0.7 all-gather.3.cloned.1.call-update
  7.9 0.0 all-gather.5.cloned.1.call-start
  8.0 0.7 all-gather.5.cloned.1.call-update
  8.7 0.0 copy-done.3
  8.7 3.0 stack.2
  11.7 0.0 copy-start.8
  11.7 0.0 copy-start.6
  11.7 5.4 %all-to-all-start = ((bf16[4,672,1152]{2,1,0:T(8,128)(2,1)}), bf16[4,672,1152]{2,1,0:T(8,128)(2,1)}, u32[]{:S(2)}, u32[]{:S(2)}) async-start(bf16[4,672,1152]{2,1,0:T(8,128)(2,1)} %stack.2), calls=%async_computation | async-start | bytes 12386304 | tf_op jit(solution)/shard_map/all_to_all | solution.py:13
  17.1 0.0 reduce-scatter.5.cloned.1.call-start
  17.8 0.0 copy-done.8
  17.8 0.0 copy-done.6
  17.8 21.3 %all_gather.12 = bf16[1,128,2688]{2,1,0:T(8,128)(2,1)S(1)} all-gather(bf16[1,16,2688]{2,1,0:T(8,128)(2,1)S(1)} %copy-done.6), channel_id=1, replica_groups=mesh['section'=4,'dp'=8] {'dp'}, dimensions={1}, use_global_device_ids=true | all-gather | bytes 774144 | tf_op jit(solution)/shard_map/all_gather | solution.py:91
  39.1 0.1 bitcast_select_fusion
  39.2 0.0 copy-start.1
  39.2 2.4 all-gather.3.cloned.1.call-done
  41.6 1.8 fusion.12
  43.4 60.6 %all-to-all-done = bf16[4,672,1152]{2,1,0:T(8,128)(2,1)} async-done(((bf16[4,672,1152]{2,1,0:T(8,128)(2,1)}), bf16[4,672,1152]{2,1,0:T(8,128)(2,1)}, u32[]{:S(2)}, u32[]{:S(2)}) %all-to-all-start) | async-done | bytes 6193184 | tf_op jit(solution)/shard_map/all_to_all | solution.py:13
  104.0 0.0 copy-done
  104.0 3.9 fusion.23
  107.9 37.5 %all-gather.5.cloned.1.call-done = bf16[1152,2688]{0,1:T(8,128)(2,1)} async-done(((bf16[1152,672]{0,1:T(8,128)(2,1)}), bf16[1152,2688]{0,1:T(8,128)(2,1)}) %all-gather.5.cloned.1.call-update) | async-done | bytes 6193168 | tf_op jit(solution)/shard_map/all_gather | solution.py:87
  145.4 3.9 fusion.6
  149.4 5.5 %convolution_convert_fusion.1 = bf16[128,2688]{1,0:T(8,128)(2,1)} fusion(bf16[128,1152]{1,0:T(8,128)(2,1)S(1)} %fusion.6, bf16[2688,1152]{1,0:T(8,128)(2,1)} %bitcast.4), kind=kOutput, calls=%fused_computation.7 | convolution fusion | flops 793067520 | bytes 7176192 | tf_op jit(solution)/shard_map/dot_general | solution.py:43
  154.9 0.0 reduce-scatter.5.cloned.1.call-update
  154.9 0.0 reduce-scatter.7.cloned.1.call-start
  155.0 0.1 dynamic-slice.6
  155.1 0.5 copy-done.9
  155.6 1.8 fusion.10
  157.3 29.5 %reduce-scatter.5.cloned.1.call-done = bf16[16,2688]{1,0:T(8,128)(2,1)} async-done(((bf16[128,2688]{1,0:T(8,128)(2,1)}), bf16[16,2688]{1,0:T(8,128)(2,1)}) %reduce-scatter.5.cloned.1.call-update) | async-done | bytes 86032 | tf_op jit(solution)/shard_map/reduce_scatter | solution.py:46
  186.8 1.6 fusion.48
  188.5 0.0 copy-done.1
  188.5 1.1 fusion.47
  189.5 2.5 collective-permute-start
  192.0 3.9 fusion.20
  195.9 0.0 collective-permute-done
  196.0 15.4 %all_gather.15 = bf16[128,2688]{1,0:T(8,128)(2,1)S(1)} all-gather(bf16[16,2688]{1,0:T(8,128)(2,1)S(1)} %collective-permute-done), channel_id=1, replica_groups=mesh['section'=4,'dp'=8] {'dp'}, dimensions={0}, use_global_device_ids=true | all-gather | bytes 774144 | tf_op jit(solution)/shard_map/all_gather | solution.py:64
  211.4 3.9 fusion.7
  215.3 0.0 copy-start.4
  215.3 0.7 copy-done.4
  216.0 5.6 %convolution_convert_fusion = bf16[128,2688]{1,0:T(8,128)(2,1)} fusion(bf16[128,1152]{1,0:T(8,128)(2,1)S(1)} %fusion.7, bf16[2688,1152]{1,0:T(8,128)(2,1)} %bitcast.4), kind=kOutput, calls=%fused_computation.6 | convolution fusion | flops 793067520 | bytes 7176192 | tf_op jit(solution)/shard_map/dot_general | solution.py:43
  221.6 0.0 reduce-scatter.7.cloned.1.call-update
  221.6 0.2 reduce-scatter.9.cloned.1.call-start
  221.9 0.0 copy-start.5
  221.9 0.0 copy-start.10
  221.9 1.9 fusion.18
  223.8 0.0 copy-done.5
  223.8 0.0 copy-done.10
  223.8 4.5 %fusion.3 = bf16[2688,1152]{1,0:T(8,128)(2,1)} fusion(f32[2688,1152]{1,0:T(8,128)S(1)} %fusion.18, bf16[128,1152]{1,0:T(8,128)(2,1)S(1)} %copy-done.5, f32[2688]{0:T(1024)S(1)} %convert_element_type.88, f32[128]{0:T(128)S(1)} %copy-done.10, bf16[1,2,128,2688]{3,2,1,0:T(8,128)(2,1)S(1)} %copy-done), kind=kOutput, calls=%fused_computation.5 | convolution fusion | flops 803389440 | bytes 19575296 | tf_op jit(solution)/shard_map/dot_general | solution.py:68
  228.3 0.0 reduce-scatter.9.cloned.1.call-update
  228.4 0.0 reduce-scatter.11.cloned.1.call-start
  228.4 1.0 copy-done.2
  229.4 1.8 fusion.33
  231.3 4.5 %fusion.2 = bf16[1152,2688]{0,1:T(8,128)(2,1)} fusion(f32[1152,2688]{0,1:T(8,128)S(1)} %fusion.33, bf16[128,2688]{1,0:T(8,128)(2,1)S(1)} %all_gather.15, f32[128,1152]{1,0:T(8,128)S(1)} %fusion.20), kind=kOutput, calls=%fused_computation.4 | convolution fusion | flops 802750464 | bytes 19857408 | tf_op jit(solution)/shard_map/dot_general | solution.py:68
  235.8 0.0 reduce-scatter.11.cloned.1.call-update
  235.8 0.6 copy-done.11
  236.5 0.1 dynamic-slice.7
  236.5 14.6 %reduce-scatter.7.cloned.1.call-done = bf16[16,2688]{1,0:T(8,128)(2,1)} async-done(((bf16[128,2688]{1,0:T(8,128)(2,1)}), bf16[16,2688]{1,0:T(8,128)(2,1)}) %reduce-scatter.7.cloned.1.call-update) | async-done | bytes 86032 | tf_op jit(solution)/shard_map/reduce_scatter | solution.py:46
  251.1 1.1 fusion.49
  252.2 0.0 copy-done.7
  252.2 38.9 %psum.7 = f32[2688]{0:T(1024)} all-reduce(f32[2688]{0:T(1024)S(1)} %add_multiply_fusion), channel_id=1, replica_groups=mesh['section'=4,'dp'=8] {'section','dp'}, use_global_device_ids=true, to_apply=%region_10.11 | all-reduce | flops 2688 | bytes 21504 | tf_op jit(solution)/shard_map/psum | solution.py:116
  291.1 1.7 fusion.50
  292.8 30.1 %reduce-scatter.9.cloned.1.call-done = bf16[672,1152]{1,0:T(8,128)(2,1)} async-done(((bf16[2688,1152]{1,0:T(8,128)(2,1)}), bf16[672,1152]{1,0:T(8,128)(2,1)}) %reduce-scatter.9.cloned.1.call-update) | async-done | bytes 1548304 | tf_op jit(solution)/shard_map/reduce_scatter | solution.py:75
  322.9 72.8 %reduce-scatter.11.cloned.1.call-done = bf16[1152,672]{0,1:T(8,128)(2,1)} async-done(((bf16[1152,2688]{0,1:T(8,128)(2,1)}), bf16[1152,672]{0,1:T(8,128)(2,1)}) %reduce-scatter.11.cloned.1.call-update) | async-done | bytes 1548304 | tf_op jit(solution)/shard_map/reduce_scatter | solution.py:78
  (12 shorter events, 0.0 us)
Async XLA Ops:
  7.2 1.5 copy-start.3
  7.2 34.5 %all-gather.3.cloned.1.call-start = ((), (), s32[]{:S(2)}) async-start(), calls=%async_computation.5 | async-start | bytes 1548288 | tf_op jit(solution)/shard_map/all_gather | solution.py:90
  7.9 137.5 %all-gather.5.cloned.1.call-start = ((), (), s32[]{:S(2)}) async-start(), calls=%async_computation.6 | async-start | bytes 7741440 | tf_op jit(solution)/shard_map/all_gather | solution.py:87
  11.7 6.1 %copy-start.8 = (bf16[2688]{0:T(1024)(128)(2,1)S(1)}, bf16[2688]{0:T(1024)(128)(2,1)}, u32[]{:S(2)}) copy-start(bf16[2688]{0:T(1024)(128)(2,1)} %param.9) | copy-start | bytes 16132
  11.7 6.1 %copy-start.6 = (bf16[1,16,2688]{2,1,0:T(8,128)(2,1)S(1)}, bf16[1,16,2688]{2,1,0:T(8,128)(2,1)}, u32[]{:S(2)}) copy-start(bf16[1,16,2688]{2,1,0:T(8,128)(2,1)} %param.7) | copy-start | bytes 258052
  11.7 92.3 %all-to-all-start = ((bf16[4,672,1152]{2,1,0:T(8,128)(2,1)}), bf16[4,672,1152]{2,1,0:T(8,128)(2,1)}, u32[]{:S(2)}, u32[]{:S(2)}) async-start(bf16[4,672,1152]{2,1,0:T(8,128)(2,1)} %stack.2), calls=%async_computation | async-start | bytes 12386304 | tf_op jit(solution)/shard_map/all_to_all | solution.py:13
  17.1 169.8 %reduce-scatter.5.cloned.1.call-start = ((), (), s32[]{:S(2)}) async-start(), calls=%async_computation.7 | async-start | bytes 774144 | tf_op jit(solution)/shard_map/reduce_scatter | solution.py:46
  39.2 149.2 %copy-start.1 = (bf16[128,2688]{1,0:T(8,128)(2,1)}, bf16[128,2688]{1,0:T(8,128)(2,1)S(1)}, u32[]{:S(2)}) copy-start(bf16[128,2688]{1,0:T(8,128)(2,1)S(1)} %bitcast_select_fusion) | copy-start | bytes 2064388
  41.6 62.3 %copy-start = (bf16[1,2,128,2688]{3,2,1,0:T(8,128)(2,1)S(1)}, bf16[1,2,128,2688]{3,2,1,0:T(8,128)(2,1)}, u32[]{:S(2)}) copy-start(bf16[1,2,128,2688]{3,2,1,0:T(8,128)(2,1)} %all-gather.3.cloned.1.call-done) | copy-start | bytes 4128772
  154.9 96.2 %reduce-scatter.7.cloned.1.call-start = ((), (), s32[]{:S(2)}) async-start(), calls=%async_computation.8 | async-start | bytes 774144 | tf_op jit(solution)/shard_map/reduce_scatter | solution.py:46
  155.1 0.5 copy-start.9
  189.5 6.4 %collective-permute-start = (bf16[16,2688]{1,0:T(8,128)(2,1)S(1)}, bf16[16,2688]{1,0:T(8,128)(2,1)S(1)}, u32[]{:S(2)}, u32[]{:S(2)}) collective-permute-start(bf16[16,2688]{1,0:T(8,128)(2,1)S(1)} %fusion.47), channel_id=1, source_target_pairs={{8,0},{16,8},{24,16},{0,24},{9,1},{17,9},{25,17},{1,25},{10,2},{18... | collective-permute-start | bytes 258056 | tf_op jit(solution)/shard_map/ppermute | solution.py:27
  215.3 0.7 copy-start.4
  221.6 101.3 %reduce-scatter.9.cloned.1.call-start = ((), (), s32[]{:S(2)}) async-start(), calls=%async_computation.9 | async-start | bytes 7741440 | tf_op jit(solution)/shard_map/reduce_scatter | solution.py:75
  221.9 1.9 copy-start.5
  221.9 1.9 copy-start.10
  228.3 1.1 copy-start.2
  228.4 167.3 %reduce-scatter.11.cloned.1.call-start = ((), (), s32[]{:S(2)}) async-start(), calls=%async_computation.10 | async-start | bytes 7741440 | tf_op jit(solution)/shard_map/reduce_scatter | solution.py:78
  235.8 0.7 copy-start.11
  235.8 16.4 %copy-start.7 = (f32[2688]{0:T(1024)S(1)}, f32[2688]{0:T(1024)}, u32[]{:S(2)}) copy-start(f32[2688]{0:T(1024)} %get-tuple-element.6) | copy-start | bytes 32260
Sparse Core Ops, SparseCore 0:
  9.6 31.9 all-gather.2
  43.5 101.8 all-gather.4
  155.0 31.7 reduce-scatter.4
  221.8 29.3 reduce-scatter.6
  254.6 68.2 reduce-scatter.8
  326.4 69.2 reduce-scatter.10
